TPU v7x, 128 devices: a whole 4x4x4 slice. The times are simulated.
128 devices in a mesh: sx: 8 (over y, core), sy: 16 (over x, z).
Axes of the slice: x: 4, y: 4, z: 4, core: 2. Of those that a mesh axis runs over, the one named last changes fastest.
Arguments:
- loads: float32 [8, 16, 1536, 256], P('sx', 'sy')
- schur_flex: float32 [8, 16, 1536, 1536], P('sx', 'sy'), as said below
- dirichlet: float32 [8, 16, 1536, 1536], P('sx', 'sy'), as said below
- coupling: float32 [8, 16, 16, 1536], P('sx', 'sy'), may hold values from -0.3125 to 0.3125
- corner_index: int32 [8, 16, 16], P('sx', 'sy'), may hold values from 0 to 512, as said below
- face_lists: int32 [8, 16, 4, 384], P('sx', 'sy'), may hold values from 0 to 383, as said below
- coarse_inverse: float32 [512, 512], P(('sx', 'sy')), as said below
Outputs:
- multipliers: float32 [8, 16, 1536, 256], P('sx', 'sy')
- residual: float32 [8, 16, 1536, 256], P('sx', 'sy')
Inputs may be any that keep to these rules, and one draw needn't show every extreme that they name: `corner_index`: each subdomain lists 4 coarse dofs for each of its four corners; 512 marks a corner on the clamped edges of the panel, which has no coarse dof; every coarse dof below 512 is named by some subdomain. `face_lists`: each face's list is a permutation of the 384 dofs of the facing face; the facing lists of two neighbouring subdomains are inverse permutations. `schur_flex`: symmetric positive definite for every subdomain. `dirichlet`: symmetric positive definite for every subdomain. `coarse_inverse`: symmetric positive definite.
All inputs are finite; a program needn't handle non-finite values.
Results may differ from a plain program's by a relative error of at most 0.00017.
Values sent between devices are 32-bit elements; how exact they have to be, the bound alone decides.
A program may use at most 128 MiB of HBM per device.

v0:
```python
import jax
import jax.numpy as jnp
from jax import lax
from jax.sharding import PartitionSpec as P

ITERS = 2


def shifted(block, axis, distance):
    devices = range(lax.axis_size(axis))
    route = [(i - distance, i) for i in devices if i - distance in devices]
    return lax.ppermute(block, axis, route)


def jump(field, face_index):
    size = field.shape[0] // 4
    width = field.shape[1]
    face_rows = field.reshape(4, size, width)
    from_low_x = shifted(face_rows[1], "sx", 1)
    from_high_x = shifted(face_rows[0], "sx", -1)
    from_low_y = shifted(face_rows[3], "sy", 1)
    from_high_y = shifted(face_rows[2], "sy", -1)
    received = jnp.stack([from_low_x, from_high_x, from_low_y, from_high_y], axis=0)
    matched = received[jnp.arange(4, dtype=jnp.int32)[:, None], face_index]
    return (face_rows - matched).reshape(4 * size, width)


def coarse_solve(coarse_rhs, stiffness_inverse_lines):
    highest = lax.Precision.HIGHEST
    total = lax.psum(coarse_rhs, ("sx", "sy"))
    mine = jnp.dot(stiffness_inverse_lines, total, precision=highest)
    return lax.all_gather(mine, ("sx", "sy"), axis=0, tiled=True)


def inner(first, second):
    return jnp.sum(first * second, axis=0)


def shards(loads, schur_flex, dirichlet, coupling, corner_index, face_lists, coarse_inverse):
    highest = lax.Precision.HIGHEST
    flex_mat = schur_flex[0, 0]
    prec_mat = dirichlet[0, 0]
    coupling_mat = coupling[0, 0]
    corners = corner_index[0, 0]
    face_index = face_lists[0, 0]
    ncoarse = coarse_inverse.shape[1]
    onehot = (corners[None, :] == jnp.arange(ncoarse, dtype=jnp.int32)[:, None]).astype(jnp.float32)

    def precondition(dual_vector):
        spread = jump(dual_vector, face_index)
        operator_applied = jnp.dot(prec_mat, spread, precision=highest)
        return 0.5 * jump(operator_applied, face_index)

    def residual_dot(residual, precond):
        return lax.psum(inner(residual, precond), ("sx", "sy"))

    force_discontinuity = jump(loads[0, 0], face_index)
    multipliers = jnp.zeros_like(force_discontinuity)
    residual = force_discontinuity
    precond = precondition(residual)
    direction = precond
    residual_inner = residual_dot(residual, precond)
    for iteration in range(ITERS):
        width = direction.shape[1]
        apply_spread = jump(direction, face_index)
        fine_part = jnp.dot(flex_mat, apply_spread, precision=highest)
        local_load = jnp.dot(coupling_mat, apply_spread, precision=highest)
        coarse_rhs = jnp.dot(onehot, local_load, precision=highest)
        coarse_sol = coarse_solve(coarse_rhs, coarse_inverse)
        filled_out = jnp.concatenate([coarse_sol, jnp.zeros((1, width), jnp.float32)], axis=0)
        picked = filled_out[corners]
        correction = lax.dot_general(
            coupling_mat, picked, (((0,), (0,)), ((), ())), precision=highest
        )
        image_dir = jump(fine_part + correction, face_index)
        step_size = residual_inner / lax.psum(inner(direction, image_dir), ("sx", "sy"))
        multipliers = multipliers + step_size * direction
        residual = residual - step_size * image_dir
        if iteration + 1 < ITERS:
            precond = precondition(residual)
            new_dot = residual_dot(residual, precond)
            direction = precond + new_dot / residual_inner * direction
            residual_inner = new_dot
    return (multipliers[None, None], residual[None, None])


def solution(mesh):
    return jax.shard_map(
        shards,
        mesh=mesh,
        in_specs=(
            P("sx", "sy", None, None),
            P("sx", "sy", None, None),
            P("sx", "sy", None, None),
            P("sx", "sy", None, None),
            P("sx", "sy", None),
            P("sx", "sy", None, None),
            P(("sx", "sy"), None),
        ),
        out_specs=(P("sx", "sy", None, None), P("sx", "sy", None, None)),
        check_vma=False,
    )
```

profile of v0, /device:TPU:1, one launch (start us, length us, event | category | flops | bytes accessed | tf_op | source)
XLA Modules:
  0.0 1103.3 jit_solution(2738854772131072380)
XLA Ops:
  8.7 4.6 collective-permute-start
  15.2 3.6 collective-permute-start.2
  22.7 3.5 collective-permute-done.2
  26.2 4.1 collective-permute-done.3
  30.4 18.0 %gather_fusion = f32[1536,256]{1,0:T(8,128)} fusion(f32[4,384,256]{2,1,0:T(8,128)S(1)} %pad_maximum_fusion, s32[1536]{0:T(1024)S(1)} %reshape.175), kind=kCustom, calls=%fused_computation | custom fusion | bytes 3158016 | tf_op jit(solution)/shard_map/gather | solution.py:24
  51.4 5.1 collective-permute-start.4
  58.5 3.4 collective-permute-start.6
  68.1 4.1 collective-permute-done.7
  72.3 18.0 %gather_fusion.1 = f32[1536,256]{1,0:T(8,128)} fusion(f32[4,384,256]{2,1,0:T(8,128)S(1)} %pad_maximum_fusion.1, s32[1536]{0:T(1024)S(1)} %reshape.175), kind=kCustom, calls=%fused_computation.1 | custom fusion | bytes 3158016 | tf_op jit(solution)/shard_map/gather | solution.py:24
  92.1 18.2 %fusion.10 = f32[1536,256]{0,1:T(8,128)S(1)} fusion(f32[1536,256]{1,0:T(8,128)S(1)} %bitcast.126, f32[1,1,1536,1536]{3,2,1,0:T(8,128)} %param.9), kind=kOutput, calls=%fused_computation.23 | convolution fusion | flops 7247757312 | bytes 12582912 | tf_op jit(solution)/shard_map/dot_general | solution.py:51
  110.3 5.9 collective-permute-start.8
  118.2 3.9 collective-permute-start.10
  126.9 4.1 collective-permute-done.11
  134.2 18.0 %gather_fusion.2 = f32[1536,256]{1,0:T(8,128)} fusion(f32[4,384,256]{2,1,0:T(8,128)S(1)} %copy.27, s32[1536]{0:T(1024)S(1)} %reshape.175), kind=kCustom, calls=%fused_computation.2 | custom fusion | bytes 3158016 | tf_op jit(solution)/shard_map/gather | solution.py:24
  157.2 6.4 collective-permute-start.12
  165.6 4.0 collective-permute-start.14
  174.3 3.9 collective-permute-done.15
  181.3 18.0 %gather_fusion.3 = f32[1536,256]{1,0:T(8,128)} fusion(f32[4,384,256]{2,1,0:T(8,128)S(1)} %copy.31, s32[1536]{0:T(1024)S(1)} %reshape.175), kind=kCustom, calls=%fused_computation.3 | custom fusion | bytes 3158016 | tf_op jit(solution)/shard_map/gather | solution.py:24
  203.9 11.6 %fusion.2 = f32[256,1536]{1,0:T(8,128)} fusion(f32[1,1,1536,1536]{3,2,1,0:T(8,128)} %param.8, f32[1536,256]{0,1:T(8,128)S(1)} %copy.32, f32[1536,256]{0,1:T(8,128)S(1)} %get-tuple-element.16), kind=kOutput, calls=%fused_computation.13 | convolution fusion | flops 7248543744 | bytes 14155776 | tf_op jit(solution)/shard_map/dot_general | solution.py:66
  215.4 139.1 %all-reduce.6.cloned.1.call-done = f32[512,256]{1,0:T(8,128)} async-done(((f32[512,256]{1,0:T(8,128)}), f32[512,256]{1,0:T(8,128)}) %all-reduce.6.cloned.1.call-update) | async-done | bytes 524304 | tf_op jit(solution)/shard_map/psum | solution.py:30
  355.9 54.6 %all-gather = f32[128,4,256]{2,1,0:T(4,128)} all-gather(f32[1,4,256]{2,1,0:T(4,128)S(1)} %convolution_bitcast_fusion.1), channel_id=1, replica_groups=mesh['sx'=8,'sy'=16] {'sx','sy'}, dimensions={0}, use_global_device_ids=true | all-gather | bytes 528384 | tf_op jit(solution)/shard_map/all_gather | solution.py:32
  435.2 4.9 collective-permute-done.19
  444.6 18.0 %gather_fusion.5 = f32[1536,256]{1,0:T(8,128)} fusion(f32[4,384,256]{2,1,0:T(8,128)S(1)} %copy.33, s32[1536]{0:T(1024)S(1)} %reshape.175), kind=kCustom, calls=%fused_computation.5 | custom fusion | bytes 3158016 | tf_op jit(solution)/shard_map/gather | solution.py:24
  465.8 3.8 multiply_reduce_fusion.2
  469.6 66.2 %all-reduce.2 = (f32[256]{0:T(256)S(1)}, f32[256]{0:T(256)S(1)}) all-reduce(f32[256]{0:T(256)S(1)} %get-tuple-element.7, f32[256]{0:T(256)S(1)} %get-tuple-element.6), channel_id=1, replica_groups=mesh['sx'=8,'sy'=16] {'sx','sy'}, use_global_device_ids=true, to_apply=%region_1.0 | all-reduce | flops 512 | bytes 4096 | tf_op jit(solution)/shard_map/psum | solution.py:55
  548.0 4.3 collective-permute-done.21
  555.3 4.1 collective-permute-done.23
  562.5 18.0 %gather_fusion.6 = f32[1536,256]{1,0:T(8,128)} fusion(f32[4,384,256]{2,1,0:T(8,128)S(1)} %copy.35, s32[1536]{0:T(1024)S(1)} %reshape.175), kind=kCustom, calls=%fused_computation.6 | custom fusion | bytes 3158016 | tf_op jit(solution)/shard_map/gather | solution.py:24
  583.7 11.3 %fusion.13 = f32[1536,256]{0,1:T(8,128)S(1)} fusion(f32[1,1,1536,1536]{3,2,1,0:T(8,128)} %param.9, f32[1536,256]{0,1:T(8,128)S(1)} %copy-done.5, f32[1536,256]{0,1:T(8,128)} %copy.36), kind=kOutput, calls=%fused_computation.24 | convolution fusion | flops 7248150528 | bytes 14155776 | tf_op jit(solution)/shard_map/dot_general | solution.py:51
  596.2 3.4 collective-permute-start.24
  605.1 3.9 collective-permute-done.25
  611.5 4.1 collective-permute-done.27
  618.8 18.0 %gather_fusion.7 = f32[1536,256]{1,0:T(8,128)} fusion(f32[4,384,256]{2,1,0:T(8,128)S(1)} %copy.37, s32[1536]{0:T(1024)S(1)} %reshape.175), kind=kCustom, calls=%fused_computation.7 | custom fusion | bytes 3158016 | tf_op jit(solution)/shard_map/gather | solution.py:24
  642.2 69.1 %psum.45 = f32[256]{0:T(256)S(1)} all-reduce(f32[256]{0:T(256)S(1)} %multiply_reduce_fusion.1), channel_id=1, replica_groups=mesh['sx'=8,'sy'=16] {'sx','sy'}, use_global_device_ids=true, to_apply=%region_6.0 | all-reduce | flops 256 | bytes 2048 | tf_op jit(solution)/shard_map/psum | solution.py:55
  714.7 3.9 collective-permute-start.28
  723.7 4.3 collective-permute-done.29
  729.7 4.1 collective-permute-done.31
  737.0 18.0 %gather_fusion.8 = f32[1536,256]{1,0:T(8,128)} fusion(f32[4,384,256]{2,1,0:T(8,128)S(1)} %copy.39, s32[1536]{0:T(1024)S(1)} %reshape.175), kind=kCustom, calls=%fused_computation.8 | custom fusion | bytes 3158016 | tf_op jit(solution)/shard_map/gather | solution.py:24
  762.1 12.2 %fusion = f32[256,1536]{1,0:T(8,128)} fusion(f32[1,1,1536,1536]{3,2,1,0:T(8,128)} %param.8, f32[1536,256]{0,1:T(8,128)S(1)} %copy-done.2, f32[1536,256]{0,1:T(8,128)} %copy.40), kind=kOutput, calls=%fused_computation.11 | convolution fusion | flops 7248150528 | bytes 14155776 | tf_op jit(solution)/shard_map/dot_general | solution.py:66
  774.3 135.6 %all-reduce.8.cloned.1.call-done = f32[512,256]{1,0:T(8,128)} async-done(((f32[512,256]{1,0:T(8,128)}), f32[512,256]{1,0:T(8,128)}) %all-reduce.8.cloned.1.call-update) | async-done | bytes 524304 | tf_op jit(solution)/shard_map/psum | solution.py:30
  911.3 54.2 %all-gather.1 = f32[128,4,256]{2,1,0:T(4,128)} all-gather(f32[1,4,256]{2,1,0:T(4,128)S(1)} %convolution_bitcast_fusion), channel_id=1, replica_groups=mesh['sx'=8,'sy'=16] {'sx','sy'}, dimensions={0}, use_global_device_ids=true | all-gather | bytes 528384 | tf_op jit(solution)/shard_map/all_gather | solution.py:32
  981.4 3.5 collective-permute-done.33
  984.9 3.8 collective-permute-done.34
  988.7 4.1 collective-permute-done.35
  995.9 18.0 %gather_fusion.10 = f32[1536,256]{1,0:T(8,128)} fusion(f32[4,384,256]{2,1,0:T(8,128)S(1)} %copy.41, s32[1536]{0:T(1024)S(1)} %reshape.175), kind=kCustom, calls=%fused_computation.10 | custom fusion | bytes 3158016 | tf_op jit(solution)/shard_map/gather | solution.py:24
  1017.0 3.4 multiply_reduce_fusion
  1020.4 66.7 %psum.47 = f32[256]{0:T(256)S(1)} all-reduce(f32[256]{0:T(256)S(1)} %get-tuple-element.12), channel_id=1, replica_groups=mesh['sx'=8,'sy'=16] {'sx','sy'}, use_global_device_ids=true, to_apply=%region_9.0 | all-reduce | flops 256 | bytes 2048 | tf_op jit(solution)/shard_map/psum | solution.py:76
  1087.1 4.1 subtract_bitcast_fusion
  (156 shorter events, 171.0 us)
Async XLA Ops:
  7.2 194.1 %copy-start = (f32[1,1,16,1536]{3,2,1,0:T(8,128)S(1)}, f32[1,1,16,1536]{3,2,1,0:T(8,128)}, u32[]{:S(2)}) copy-start(f32[1,1,16,1536]{3,2,1,0:T(8,128)} %param.10) | copy-start | bytes 294916
  7.2 12.9 %copy-start.19 = (s32[1,1,4,384]{3,2,1,0:T(4,128)S(1)}, s32[1,1,4,384]{3,2,1,0:T(4,128)}, u32[]{:S(2)}) copy-start(s32[1,1,4,384]{3,2,1,0:T(4,128)} %param.12) | copy-start | bytes 18436
  7.2 347.3 %all-reduce.6.cloned.1.call-start = ((), (), s32[]{:S(2)}) async-start(), calls=%async_computation | async-start | bytes 1048576 | tf_op jit(solution)/shard_map/psum | solution.py:30
  8.7 11.4 %collective-permute-start = (f32[384,256]{1,0:T(8,128)S(1)}, f32[384,256]{1,0:T(8,128)S(1)}, u32[]{:S(2)}, u32[]{:S(2)}) collective-permute-start(f32[384,256]{1,0:T(8,128)S(1)} %get-tuple-element.49), channel_id=1, source_target_pairs={{0,16},{16,32},{32,48},{48,64},{64,80},{80,96},{96,112},{1,17},{17... | collective-permute-start | bytes 1179656 | tf_op jit(solution)/shard_map/ppermute | solution.py:12
  13.3 9.4 collective-permute-start.1
  15.2 11.0 collective-permute-start.2
  18.8 11.5 %collective-permute-start.3 = (f32[384,256]{1,0:T(8,128)S(1)}, f32[384,256]{1,0:T(8,128)S(1)}, u32[]{:S(2)}, u32[]{:S(2)}) collective-permute-start(f32[384,256]{1,0:T(8,128)S(1)} %get-tuple-element.52), channel_id=1, source_target_pairs={{1,0},{2,1},{3,2},{4,3},{5,4},{6,5},{7,6},{8,7},{9,8},{10,9},{11,1... | collective-permute-start | bytes 1179656 | tf_op jit(solution)/shard_map/ppermute | solution.py:12
  30.4 18.0 %copy-start.10 = (f32[1,1,1536,256]{3,2,1,0:T(8,128)S(1)}, f32[1,1,1536,256]{3,2,1,0:T(8,128)}, u32[]{:S(2)}) copy-start(f32[1,1,1536,256]{3,2,1,0:T(8,128)} %param.7) | copy-start | bytes 4718596
  51.4 11.8 %collective-permute-start.4 = (f32[384,256]{1,0:T(8,128)S(1)}, f32[384,256]{1,0:T(8,128)S(1)}, u32[]{:S(2)}, u32[]{:S(2)}) collective-permute-start(f32[384,256]{1,0:T(8,128)S(1)} %get-tuple-element.45), channel_id=1, source_target_pairs={{0,16},{16,32},{32,48},{48,64},{64,80},{80,96},{96,112},{1,17},{17... | collective-permute-start | bytes 1179656 | tf_op jit(solution)/shard_map/ppermute | solution.py:12
  56.6 9.4 collective-permute-start.5
  58.5 9.6 collective-permute-start.6
  61.9 10.3 collective-permute-start.7
  72.3 18.0 %copy-start.13 = (f32[4,384,256]{2,1,0:T(8,128)S(1)}, f32[4,384,256]{2,1,0:T(8,128)}, u32[]{:S(2)}) copy-start(f32[4,384,256]{2,1,0:T(8,128)} %copy-done.12) | copy-start | bytes 4718596
  110.3 13.3 %collective-permute-start.8 = (f32[384,256]{0,1:T(8,128)S(1)}, f32[384,256]{0,1:T(8,128)S(1)}, u32[]{:S(2)}, u32[]{:S(2)}) collective-permute-start(f32[384,256]{0,1:T(8,128)S(1)} %get-tuple-element.41), channel_id=1, source_target_pairs={{0,16},{16,32},{32,48},{48,64},{64,80},{80,96},{96,112},{1,17},{17... | collective-permute-start | bytes 1179656 | tf_op jit(solution)/shard_map/ppermute | solution.py:12
  116.3 9.4 collective-permute-start.9
  118.2 8.7 collective-permute-start.10
  122.1 8.9 collective-permute-start.11
  157.1 13.8 %copy-start.20 = (s32[1,1,16]{2,1,0:T(1,128)S(1)}, s32[1,1,16]{2,1,0:T(1,128)}, u32[]{:S(2)}) copy-start(s32[1,1,16]{2,1,0:T(1,128)} %param.11) | copy-start | bytes 196
  157.2 13.8 %collective-permute-start.12 = (f32[384,256]{0,1:T(8,128)S(1)}, f32[384,256]{0,1:T(8,128)S(1)}, u32[]{:S(2)}, u32[]{:S(2)}) collective-permute-start(f32[384,256]{0,1:T(8,128)S(1)} %get-tuple-element.37), channel_id=1, source_target_pairs={{0,16},{16,32},{32,48},{48,64},{64,80},{80,96},{96,112},{1,17},{17... | collective-permute-start | bytes 1179656 | tf_op jit(solution)/shard_map/ppermute | solution.py:12
  163.7 9.4 collective-permute-start.13
  165.6 8.7 collective-permute-start.14
  169.6 8.6 collective-permute-start.15
  203.8 150.7 %copy-start.18 = (f32[4,512]{1,0:T(4,128)S(1)}, f32[4,512]{1,0:T(4,128)}, u32[]{:S(2)}) copy-start(f32[4,512]{1,0:T(4,128)} %param.13) | copy-start | bytes 24580
  203.8 706.1 %all-reduce.8.cloned.1.call-start = ((), (), s32[]{:S(2)}) async-start(), calls=%async_computation.1 | async-start | bytes 1048576 | tf_op jit(solution)/shard_map/psum | solution.py:30
  215.4 200.5 %copy-start.16 = (f32[256,1536]{1,0:T(8,128)S(1)}, f32[256,1536]{1,0:T(8,128)}, u32[]{:S(2)}) copy-start(f32[256,1536]{1,0:T(8,128)} %fusion.2) | copy-start | bytes 4718596
  417.4 10.8 copy-start.11
  419.1 13.7 %collective-permute-start.16 = (f32[384,256]{0,1:T(8,128)}, f32[384,256]{0,1:T(8,128)}, u32[]{:S(2)}, u32[]{:S(2)}) collective-permute-start(f32[384,256]{0,1:T(8,128)} %get-tuple-element.33), channel_id=1, source_target_pairs={{0,16},{16,32},{32,48},{48,64},{64,80},{80,96},{96,112},{1,17},{17... | collective-permute-start | bytes 1179656 | tf_op jit(solution)/shard_map/ppermute | solution.py:12
  421.0 11.8 %collective-permute-start.17 = (f32[384,256]{0,1:T(8,128)}, f32[384,256]{0,1:T(8,128)}, u32[]{:S(2)}, u32[]{:S(2)}) collective-permute-start(f32[384,256]{0,1:T(8,128)} %get-tuple-element.36), channel_id=1, source_target_pairs={{16,0},{32,16},{48,32},{64,48},{80,64},{96,80},{112,96},{17,1},{33... | collective-permute-start | bytes 1179656 | tf_op jit(solution)/shard_map/ppermute | solution.py:12
  424.2 11.1 %collective-permute-start.18 = (f32[384,256]{0,1:T(8,128)}, f32[384,256]{0,1:T(8,128)}, u32[]{:S(2)}, u32[]{:S(2)}) collective-permute-start(f32[384,256]{0,1:T(8,128)} %get-tuple-element.35), channel_id=1, source_target_pairs={{0,1},{1,2},{2,3},{3,4},{4,5},{5,6},{6,7},{7,8},{8,9},{9,10},{10,1... | collective-permute-start | bytes 1179656 | tf_op jit(solution)/shard_map/ppermute | solution.py:12
  426.9 13.2 %collective-permute-start.19 = (f32[384,256]{0,1:T(8,128)}, f32[384,256]{0,1:T(8,128)}, u32[]{:S(2)}, u32[]{:S(2)}) collective-permute-start(f32[384,256]{0,1:T(8,128)} %get-tuple-element.34), channel_id=1, source_target_pairs={{1,0},{2,1},{3,2},{4,3},{5,4},{6,5},{7,6},{8,7},{9,8},{10,9},{11,1... | collective-permute-start | bytes 1179656 | tf_op jit(solution)/shard_map/ppermute | solution.py:12
  539.6 8.3 collective-permute-start.20
  542.9 9.4 collective-permute-start.21
  544.8 10.5 collective-permute-start.22
  546.5 12.9 %collective-permute-start.23 = (f32[384,256]{0,1:T(8,128)S(1)}, f32[384,256]{0,1:T(8,128)S(1)}, u32[]{:S(2)}, u32[]{:S(2)}) collective-permute-start(f32[384,256]{0,1:T(8,128)S(1)} %get-tuple-element.30), channel_id=1, source_target_pairs={{1,0},{2,1},{3,2},{4,3},{5,4},{6,5},{7,6},{8,7},{9,8},{10,9},{11,1... | collective-permute-start | bytes 1179656 | tf_op jit(solution)/shard_map/ppermute | solution.py:12
  580.5 3.2 copy-start.5
  596.2 9.0 collective-permute-start.24
  599.6 9.4 collective-permute-start.25
  601.5 9.9 collective-permute-start.26
  603.8 11.8 %collective-permute-start.27 = (f32[384,256]{0,1:T(8,128)S(1)}, f32[384,256]{0,1:T(8,128)S(1)}, u32[]{:S(2)}, u32[]{:S(2)}) collective-permute-start(f32[384,256]{0,1:T(8,128)S(1)} %get-tuple-element.26), channel_id=1, source_target_pairs={{1,0},{2,1},{3,2},{4,3},{5,4},{6,5},{7,6},{8,7},{9,8},{10,9},{11,1... | collective-permute-start | bytes 1179656 | tf_op jit(solution)/shard_map/ppermute | solution.py:12
  714.7 9.0 collective-permute-start.28
  718.5 9.4 collective-permute-start.29
  720.5 9.2 collective-permute-start.30
  722.1 11.7 %collective-permute-start.31 = (f32[384,256]{0,1:T(8,128)S(1)}, f32[384,256]{0,1:T(8,128)S(1)}, u32[]{:S(2)}, u32[]{:S(2)}) collective-permute-start(f32[384,256]{0,1:T(8,128)S(1)} %get-tuple-element.22), channel_id=1, source_target_pairs={{1,0},{2,1},{3,2},{4,3},{5,4},{6,5},{7,6},{8,7},{9,8},{10,9},{11,1... | collective-permute-start | bytes 1179656 | tf_op jit(solution)/shard_map/ppermute | solution.py:12
  774.3 196.7 %copy-start.15 = (f32[256,1536]{1,0:T(8,128)S(1)}, f32[256,1536]{1,0:T(8,128)}, u32[]{:S(2)}) copy-start(f32[256,1536]{1,0:T(8,128)} %fusion) | copy-start | bytes 4718596
  973.6 7.8 collective-permute-start.32
  975.5 9.4 collective-permute-start.33
  977.9 10.7 collective-permute-start.34
  979.9 12.9 %collective-permute-start.35 = (f32[384,256]{0,1:T(8,128)S(1)}, f32[384,256]{0,1:T(8,128)S(1)}, u32[]{:S(2)}, u32[]{:S(2)}) collective-permute-start(f32[384,256]{0,1:T(8,128)S(1)} %get-tuple-element.18), channel_id=1, source_target_pairs={{1,0},{2,1},{3,2},{4,3},{5,4},{6,5},{7,6},{8,7},{9,8},{10,9},{11,1... | collective-permute-start | bytes 1179656 | tf_op jit(solution)/shard_map/ppermute | solution.py:12
  (11 other events, 23.2 us)
Sparse Core Ops, SparseCore 0:
  203.9 150.5 all-reduce.5
  762.2 147.6 all-reduce.7
where the time goes:
time: 1110 us; the launch traced here: 1100 us
  waiting for transfers between devices  359 us (32%)
  blocking collectives  311 us (28%)
  local copies, waits for them, and re-layouts  225 us (20%)
  starting transfers between devices  93.2 us (8%)
  matrix products  65.3 us (6%)
  other arithmetic  34.2 us (3%)
  between operations  15.2 us (1%)
    psum x2, waiting for transfers between devices, coarse_solve(): total = lax.psum(coarse_rhs, ('sx', 'sy'))  275 us
    gather x17, local copies, waits for them, and re-layouts, jump(): matched = received[jnp.arange(4, dtype=jnp.int32)[:, None], face_index]  186 us
    psum x2, blocking collectives, residual_dot(): return lax.psum(inner(residual, precond), ('sx', 'sy'))  135 us
    all_gather x2, blocking collectives, coarse_solve(): return lax.all_gather(mine, ('sx', 'sy'), axis=0, tiled=True)  109 us
    ppermute x36, starting transfers between devices, shifted(): return lax.ppermute(block, axis, route)  93.1 us
    ppermute x36, waiting for transfers between devices, shifted(): return lax.ppermute(block, axis, route)  84.4 us
    psum x1, blocking collectives, shards(): lax.psum(inner(direction, image_dir), ('sx', 'sy'))  66.7 us
    dot_general x2, matrix products, precondition(): operator_applied = jnp.dot(prec_mat, spread, precision=highest)  29.5 us
  transfers between devices with their start and end apart: 38, of which 28 were waited for; matrix products, arithmetic and copies ran while one was open for 3% of the time, Pallas kernels for 0%

commit v1 on v0

--- a/solution.py
+++ b/solution.py
@@ -29,7 +29,9 @@
     highest = lax.Precision.HIGHEST
     total = lax.psum(coarse_rhs, ("sx", "sy"))
     mine = jnp.dot(stiffness_inverse_lines, total, precision=highest)
-    return lax.all_gather(mine, ("sx", "sy"), axis=0, tiled=True)
+    return jnp.concatenate(
+        lax.all_to_all(jnp.stack([mine] * lax.axis_size(("sx", "sy"))), ("sx", "sy"), 0, 0), axis=0
+    )
 
 
 def inner(first, second):

time: 1110 us -> 1050 us (0.946)
  blocking collectives: 311 us -> 200 us
  waiting for transfers between devices: 359 us -> 384 us
  starting transfers between devices: 93.2 us -> 110 us
    all_gather x2 -> x0, blocking collectives: 109 us -> none  [coarse_solve(): return lax.all_gather(mine, ('sx', 'sy'), axis=0, tiled=True)]
    psum x2, waiting for transfers between devices: 275 us -> 298 us  [coarse_solve(): total = lax.psum(coarse_rhs, ('sx', 'sy'))]
    all_to_all x0 -> x2, starting transfers between devices: none -> 14.5 us  [coarse_solve(): lax.all_to_all(jnp.stack([mine] * lax.axis_size(('sx', 'sy'))), ('sx', 's...]
  transfers between devices with their start and end apart: 38 -> 40, of which waited for: 28 -> 30; matrix products, arithmetic and copies ran while one was open for 3% -> 3% of each run, Pallas kernels for 0% -> 0%
where the time goes in v1:
time: 1050 us; the launch traced here: 1040 us
  waiting for transfers between devices  384 us (37%)
  local copies, waits for them, and re-layouts  227 us (22%)
  blocking collectives  200 us (19%)
  starting transfers between devices  110 us (10%)
  matrix products  65.3 us (6%)
  other arithmetic  34.2 us (3%)
  between operations  15.3 us (1%)
    psum x2, waiting for transfers between devices, coarse_solve(): total = lax.psum(coarse_rhs, ('sx', 'sy'))  298 us
    gather x17, local copies, waits for them, and re-layouts, jump(): matched = received[jnp.arange(4, dtype=jnp.int32)[:, None], face_index]  186 us
    psum x2, blocking collectives, residual_dot(): return lax.psum(inner(residual, precond), ('sx', 'sy'))  134 us
    ppermute x36, starting transfers between devices, shifted(): return lax.ppermute(block, axis, route)  95.5 us
    ppermute x36, waiting for transfers between devices, shifted(): return lax.ppermute(block, axis, route)  83.9 us
    psum x1, blocking collectives, shards(): lax.psum(inner(direction, image_dir), ('sx', 'sy'))  66.3 us
    dot_general x2, matrix products, precondition(): operator_applied = jnp.dot(prec_mat, spread, precision=highest)  29.5 us
    dot_general x2, matrix products, shards(): fine_part = jnp.dot(flex_mat, apply_spread, precision=highest)  23.7 us
  transfers between devices with their start and end apart: 40, of which 30 were waited for; matrix products, arithmetic and copies ran while one was open for 3% of the time, Pallas kernels for 0%

profile of v1, /device:TPU:1, one launch (start us, length us, event | category | flops | bytes accessed | tf_op | source)
XLA Modules:
  0.0 1036.5 jit_solution(4278924639344781474)
XLA Ops:
  8.7 4.6 collective-permute-start
  15.2 3.6 collective-permute-start.2
  22.7 3.5 collective-permute-done.2
  26.2 4.1 collective-permute-done.3
  30.4 18.0 %gather_fusion = f32[1536,256]{1,0:T(8,128)} fusion(f32[4,384,256]{2,1,0:T(8,128)S(1)} %pad_maximum_fusion, s32[1536]{0:T(1024)S(1)} %reshape.187), kind=kCustom, calls=%fused_computation | custom fusion | bytes 3158016 | tf_op jit(solution)/shard_map/gather | solution.py:24
  51.4 5.1 collective-permute-start.4
  58.5 3.4 collective-permute-start.6
  68.1 4.1 collective-permute-done.7
  72.3 18.0 %gather_fusion.1 = f32[1536,256]{1,0:T(8,128)} fusion(f32[4,384,256]{2,1,0:T(8,128)S(1)} %pad_maximum_fusion.1, s32[1536]{0:T(1024)S(1)} %reshape.187), kind=kCustom, calls=%fused_computation.1 | custom fusion | bytes 3158016 | tf_op jit(solution)/shard_map/gather | solution.py:24
  92.1 18.2 %fusion.10 = f32[1536,256]{0,1:T(8,128)S(1)} fusion(f32[1536,256]{1,0:T(8,128)S(1)} %bitcast.122, f32[1,1,1536,1536]{3,2,1,0:T(8,128)} %param.9), kind=kOutput, calls=%fused_computation.23 | convolution fusion | flops 7247757312 | bytes 12582912 | tf_op jit(solution)/shard_map/dot_general | solution.py:53
  110.4 5.9 collective-permute-start.8
  118.2 3.9 collective-permute-start.10
  126.9 4.1 collective-permute-done.11
  134.2 18.0 %gather_fusion.2 = f32[1536,256]{1,0:T(8,128)} fusion(f32[4,384,256]{2,1,0:T(8,128)S(1)} %copy.9, s32[1536]{0:T(1024)S(1)} %reshape.187), kind=kCustom, calls=%fused_computation.2 | custom fusion | bytes 3158016 | tf_op jit(solution)/shard_map/gather | solution.py:24
  157.2 6.4 collective-permute-start.12
  165.6 4.0 collective-permute-start.14
  174.3 3.9 collective-permute-done.15
  181.3 18.0 %gather_fusion.3 = f32[1536,256]{1,0:T(8,128)} fusion(f32[4,384,256]{2,1,0:T(8,128)S(1)} %copy.13, s32[1536]{0:T(1024)S(1)} %reshape.187), kind=kCustom, calls=%fused_computation.3 | custom fusion | bytes 3158016 | tf_op jit(solution)/shard_map/gather | solution.py:24
  203.8 150.7 %all-reduce.6.cloned.1.call-done = f32[512,256]{1,0:T(8,128)} async-done(((f32[512,256]{1,0:T(8,128)}), f32[512,256]{1,0:T(8,128)}) %all-reduce.6.cloned.1.call-update) | async-done | bytes 524304 | tf_op jit(solution)/shard_map/psum | solution.py:30
  356.8 7.2 all-to-all-start
  364.5 11.6 %fusion.2 = f32[256,1536]{1,0:T(8,128)} fusion(f32[1,1,1536,1536]{3,2,1,0:T(8,128)} %param.8, f32[1536,256]{0,1:T(8,128)S(1)} %copy.14, f32[1536,256]{0,1:T(8,128)S(1)} %get-tuple-element.14), kind=kOutput, calls=%fused_computation.13 | convolution fusion | flops 7248543744 | bytes 14155776 | tf_op jit(solution)/shard_map/dot_general | solution.py:68
  385.7 3.4 collective-permute-start.16
  402.5 5.0 collective-permute-done.19
  412.0 18.0 %gather_fusion.5 = f32[1536,256]{1,0:T(8,128)} fusion(f32[4,384,256]{2,1,0:T(8,128)S(1)} %copy.15, s32[1536]{0:T(1024)S(1)} %reshape.187), kind=kCustom, calls=%fused_computation.5 | custom fusion | bytes 3158016 | tf_op jit(solution)/shard_map/gather | solution.py:24
  433.2 3.8 multiply_reduce_fusion.2
  437.0 65.6 %all-reduce.2 = (f32[256]{0:T(256)S(1)}, f32[256]{0:T(256)S(1)}) all-reduce(f32[256]{0:T(256)S(1)} %get-tuple-element.5, f32[256]{0:T(256)S(1)} %get-tuple-element.4), channel_id=1, replica_groups=mesh['sx'=8,'sy'=16] {'sx','sy'}, use_global_device_ids=true, to_apply=%region_1.0 | all-reduce | flops 512 | bytes 4096 | tf_op jit(solution)/shard_map/psum | solution.py:57
  514.5 3.9 collective-permute-done.21
  521.3 4.2 collective-permute-done.23
  528.6 18.0 %gather_fusion.6 = f32[1536,256]{1,0:T(8,128)} fusion(f32[4,384,256]{2,1,0:T(8,128)S(1)} %copy.17, s32[1536]{0:T(1024)S(1)} %reshape.187), kind=kCustom, calls=%fused_computation.6 | custom fusion | bytes 3158016 | tf_op jit(solution)/shard_map/gather | solution.py:24
  549.8 11.3 %fusion.13 = f32[1536,256]{0,1:T(8,128)S(1)} fusion(f32[1,1,1536,1536]{3,2,1,0:T(8,128)} %param.9, f32[1536,256]{0,1:T(8,128)S(1)} %copy-done.5, f32[1536,256]{0,1:T(8,128)} %copy.18), kind=kOutput, calls=%fused_computation.24 | convolution fusion | flops 7248150528 | bytes 14155776 | tf_op jit(solution)/shard_map/dot_general | solution.py:53
  571.5 3.5 collective-permute-done.25
  575.0 3.5 collective-permute-done.26
  578.5 4.1 collective-permute-done.27
  585.8 18.0 %gather_fusion.7 = f32[1536,256]{1,0:T(8,128)} fusion(f32[4,384,256]{2,1,0:T(8,128)S(1)} %copy.19, s32[1536]{0:T(1024)S(1)} %reshape.187), kind=kCustom, calls=%fused_computation.7 | custom fusion | bytes 3158016 | tf_op jit(solution)/shard_map/gather | solution.py:24
  609.2 68.0 %psum.45 = f32[256]{0:T(256)S(1)} all-reduce(f32[256]{0:T(256)S(1)} %multiply_reduce_fusion.1), channel_id=1, replica_groups=mesh['sx'=8,'sy'=16] {'sx','sy'}, use_global_device_ids=true, to_apply=%region_6.0 | all-reduce | flops 256 | bytes 2048 | tf_op jit(solution)/shard_map/psum | solution.py:57
  680.6 4.0 collective-permute-start.28
  689.3 4.6 collective-permute-done.29
  695.7 4.1 collective-permute-done.31
  703.0 17.9 %gather_fusion.8 = f32[1536,256]{1,0:T(8,128)} fusion(f32[4,384,256]{2,1,0:T(8,128)S(1)} %copy.21, s32[1536]{0:T(1024)S(1)} %reshape.187), kind=kCustom, calls=%fused_computation.8 | custom fusion | bytes 3158016 | tf_op jit(solution)/shard_map/gather | solution.py:24
  728.1 147.7 %all-reduce.8.cloned.1.call-done = f32[512,256]{1,0:T(8,128)} async-done(((f32[512,256]{1,0:T(8,128)}), f32[512,256]{1,0:T(8,128)}) %all-reduce.8.cloned.1.call-update) | async-done | bytes 524304 | tf_op jit(solution)/shard_map/psum | solution.py:30
  878.0 7.3 all-to-all-start.1
  885.3 12.2 %fusion = f32[256,1536]{1,0:T(8,128)} fusion(f32[1,1,1536,1536]{3,2,1,0:T(8,128)} %param.8, f32[1536,256]{0,1:T(8,128)S(1)} %copy-done.2, f32[1536,256]{0,1:T(8,128)} %copy.22), kind=kOutput, calls=%fused_computation.11 | convolution fusion | flops 7248150528 | bytes 14155776 | tf_op jit(solution)/shard_map/dot_general | solution.py:68
  906.5 3.4 collective-permute-start.32
  922.3 4.1 collective-permute-done.35
  929.5 18.0 %gather_fusion.10 = f32[1536,256]{1,0:T(8,128)} fusion(f32[4,384,256]{2,1,0:T(8,128)S(1)} %copy.23, s32[1536]{0:T(1024)S(1)} %reshape.187), kind=kCustom, calls=%fused_computation.10 | custom fusion | bytes 3158016 | tf_op jit(solution)/shard_map/gather | solution.py:24
  950.6 3.4 multiply_reduce_fusion
  954.0 66.3 %psum.47 = f32[256]{0:T(256)S(1)} all-reduce(f32[256]{0:T(256)S(1)} %get-tuple-element.10), channel_id=1, replica_groups=mesh['sx'=8,'sy'=16] {'sx','sy'}, use_global_device_ids=true, to_apply=%region_9.0 | all-reduce | flops 256 | bytes 2048 | tf_op jit(solution)/shard_map/psum | solution.py:78
  1020.4 4.1 subtract_bitcast_fusion
  (160 shorter events, 177.4 us)
Async XLA Ops:
  7.2 194.0 %copy-start = (f32[1,1,16,1536]{3,2,1,0:T(8,128)S(1)}, f32[1,1,16,1536]{3,2,1,0:T(8,128)}, u32[]{:S(2)}) copy-start(f32[1,1,16,1536]{3,2,1,0:T(8,128)} %param.10) | copy-start | bytes 294916
  7.2 12.9 %copy-start.19 = (s32[1,1,4,384]{3,2,1,0:T(4,128)S(1)}, s32[1,1,4,384]{3,2,1,0:T(4,128)}, u32[]{:S(2)}) copy-start(s32[1,1,4,384]{3,2,1,0:T(4,128)} %param.12) | copy-start | bytes 18436
  7.2 347.3 %all-reduce.6.cloned.1.call-start = ((), (), s32[]{:S(2)}) async-start(), calls=%async_computation.2 | async-start | bytes 1048576 | tf_op jit(solution)/shard_map/psum | solution.py:30
  8.7 11.4 %collective-permute-start = (f32[384,256]{1,0:T(8,128)S(1)}, f32[384,256]{1,0:T(8,128)S(1)}, u32[]{:S(2)}, u32[]{:S(2)}) collective-permute-start(f32[384,256]{1,0:T(8,128)S(1)} %get-tuple-element.47), channel_id=1, source_target_pairs={{0,16},{16,32},{32,48},{48,64},{64,80},{80,96},{96,112},{1,17},{17... | collective-permute-start | bytes 1179656 | tf_op jit(solution)/shard_map/ppermute | solution.py:12
  13.3 9.4 collective-permute-start.1
  15.2 11.0 %collective-permute-start.2 = (f32[384,256]{1,0:T(8,128)S(1)}, f32[384,256]{1,0:T(8,128)S(1)}, u32[]{:S(2)}, u32[]{:S(2)}) collective-permute-start(f32[384,256]{1,0:T(8,128)S(1)} %get-tuple-element.48), channel_id=1, source_target_pairs={{0,1},{1,2},{2,3},{3,4},{4,5},{5,6},{6,7},{7,8},{8,9},{9,10},{10,1... | collective-permute-start | bytes 1179656 | tf_op jit(solution)/shard_map/ppermute | solution.py:12
  18.8 11.5 %collective-permute-start.3 = (f32[384,256]{1,0:T(8,128)S(1)}, f32[384,256]{1,0:T(8,128)S(1)}, u32[]{:S(2)}, u32[]{:S(2)}) collective-permute-start(f32[384,256]{1,0:T(8,128)S(1)} %get-tuple-element.50), channel_id=1, source_target_pairs={{1,0},{2,1},{3,2},{4,3},{5,4},{6,5},{7,6},{8,7},{9,8},{10,9},{11,1... | collective-permute-start | bytes 1179656 | tf_op jit(solution)/shard_map/ppermute | solution.py:12
  30.4 18.0 %copy-start.10 = (f32[1,1,1536,256]{3,2,1,0:T(8,128)S(1)}, f32[1,1,1536,256]{3,2,1,0:T(8,128)}, u32[]{:S(2)}) copy-start(f32[1,1,1536,256]{3,2,1,0:T(8,128)} %param.7) | copy-start | bytes 4718596
  51.4 11.8 %collective-permute-start.4 = (f32[384,256]{1,0:T(8,128)S(1)}, f32[384,256]{1,0:T(8,128)S(1)}, u32[]{:S(2)}, u32[]{:S(2)}) collective-permute-start(f32[384,256]{1,0:T(8,128)S(1)} %get-tuple-element.43), channel_id=1, source_target_pairs={{0,16},{16,32},{32,48},{48,64},{64,80},{80,96},{96,112},{1,17},{17... | collective-permute-start | bytes 1179656 | tf_op jit(solution)/shard_map/ppermute | solution.py:12
  56.6 9.4 collective-permute-start.5
  58.5 9.6 collective-permute-start.6
  61.9 10.3 collective-permute-start.7
  72.3 18.0 %copy-start.13 = (f32[4,384,256]{2,1,0:T(8,128)S(1)}, f32[4,384,256]{2,1,0:T(8,128)}, u32[]{:S(2)}) copy-start(f32[4,384,256]{2,1,0:T(8,128)} %copy-done.12) | copy-start | bytes 4718596
  110.4 13.3 %collective-permute-start.8 = (f32[384,256]{0,1:T(8,128)S(1)}, f32[384,256]{0,1:T(8,128)S(1)}, u32[]{:S(2)}, u32[]{:S(2)}) collective-permute-start(f32[384,256]{0,1:T(8,128)S(1)} %get-tuple-element.39), channel_id=1, source_target_pairs={{0,16},{16,32},{32,48},{48,64},{64,80},{80,96},{96,112},{1,17},{17... | collective-permute-start | bytes 1179656 | tf_op jit(solution)/shard_map/ppermute | solution.py:12
  116.3 9.4 collective-permute-start.9
  118.2 8.7 collective-permute-start.10
  122.1 8.9 collective-permute-start.11
  157.2 13.7 %collective-permute-start.12 = (f32[384,256]{0,1:T(8,128)S(1)}, f32[384,256]{0,1:T(8,128)S(1)}, u32[]{:S(2)}, u32[]{:S(2)}) collective-permute-start(f32[384,256]{0,1:T(8,128)S(1)} %get-tuple-element.35), channel_id=1, source_target_pairs={{0,16},{16,32},{32,48},{48,64},{64,80},{80,96},{96,112},{1,17},{17... | collective-permute-start | bytes 1179656 | tf_op jit(solution)/shard_map/ppermute | solution.py:12
  163.6 9.4 collective-permute-start.13
  165.6 8.7 collective-permute-start.14
  169.6 8.6 collective-permute-start.15
  201.2 153.3 %copy-start.18 = (f32[4,512]{1,0:T(4,128)S(1)}, f32[4,512]{1,0:T(4,128)}, u32[]{:S(2)}) copy-start(f32[4,512]{1,0:T(4,128)} %param.13) | copy-start | bytes 24580
  356.8 20.3 %all-to-all-start = ((f32[128,4,256]{2,1,0:T(4,128)}), f32[128,4,256]{2,1,0:T(4,128)}, u32[]{:S(2)}, u32[]{:S(2)}) async-start(f32[128,4,256]{2,1,0:T(4,128)} %stack.114), calls=%async_computation | async-start | bytes 1048576 | tf_op jit(solution)/shard_map/all_to_all | solution.py:33
  364.0 511.7 %all-reduce.8.cloned.1.call-start = ((), (), s32[]{:S(2)}) async-start(), calls=%async_computation.3 | async-start | bytes 1048576 | tf_op jit(solution)/shard_map/psum | solution.py:30
  376.1 6.5 copy-start.16
  384.1 11.7 %copy-start.11 = (f32[1,1,1536,256]{3,2,1,0:T(8,128)S(1)}, f32[1,1,1536,256]{3,2,1,0:T(8,128)}, u32[]{:S(2)}) copy-start(f32[1,1,1536,256]{3,2,1,0:T(8,128)} %param.7) | copy-start | bytes 4718596
  385.7 14.6 %collective-permute-start.16 = (f32[384,256]{0,1:T(8,128)}, f32[384,256]{0,1:T(8,128)}, u32[]{:S(2)}, u32[]{:S(2)}) collective-permute-start(f32[384,256]{0,1:T(8,128)} %get-tuple-element.31), channel_id=1, source_target_pairs={{0,16},{16,32},{32,48},{48,64},{64,80},{80,96},{96,112},{1,17},{17... | collective-permute-start | bytes 1179656 | tf_op jit(solution)/shard_map/ppermute | solution.py:12
  389.1 11.2 %collective-permute-start.17 = (f32[384,256]{0,1:T(8,128)}, f32[384,256]{0,1:T(8,128)}, u32[]{:S(2)}, u32[]{:S(2)}) collective-permute-start(f32[384,256]{0,1:T(8,128)} %get-tuple-element.34), channel_id=1, source_target_pairs={{16,0},{32,16},{48,32},{64,48},{80,64},{96,80},{112,96},{17,1},{33... | collective-permute-start | bytes 1179656 | tf_op jit(solution)/shard_map/ppermute | solution.py:12
  391.1 11.5 %collective-permute-start.18 = (f32[384,256]{0,1:T(8,128)}, f32[384,256]{0,1:T(8,128)}, u32[]{:S(2)}, u32[]{:S(2)}) collective-permute-start(f32[384,256]{0,1:T(8,128)} %get-tuple-element.33), channel_id=1, source_target_pairs={{0,1},{1,2},{2,3},{3,4},{4,5},{5,6},{6,7},{7,8},{8,9},{9,10},{10,1... | collective-permute-start | bytes 1179656 | tf_op jit(solution)/shard_map/ppermute | solution.py:12
  394.4 13.1 %collective-permute-start.19 = (f32[384,256]{0,1:T(8,128)}, f32[384,256]{0,1:T(8,128)}, u32[]{:S(2)}, u32[]{:S(2)}) collective-permute-start(f32[384,256]{0,1:T(8,128)} %get-tuple-element.32), channel_id=1, source_target_pairs={{1,0},{2,1},{3,2},{4,3},{5,4},{6,5},{7,6},{8,7},{9,8},{10,9},{11,1... | collective-permute-start | bytes 1179656 | tf_op jit(solution)/shard_map/ppermute | solution.py:12
  506.4 8.0 collective-permute-start.20
  508.9 9.4 collective-permute-start.21
  510.9 10.5 %collective-permute-start.22 = (f32[384,256]{0,1:T(8,128)S(1)}, f32[384,256]{0,1:T(8,128)S(1)}, u32[]{:S(2)}, u32[]{:S(2)}) collective-permute-start(f32[384,256]{0,1:T(8,128)S(1)} %get-tuple-element.29), channel_id=1, source_target_pairs={{0,1},{1,2},{2,3},{3,4},{4,5},{5,6},{6,7},{7,8},{8,9},{9,10},{10,1... | collective-permute-start | bytes 1179656 | tf_op jit(solution)/shard_map/ppermute | solution.py:12
  513.0 12.5 %collective-permute-start.23 = (f32[384,256]{0,1:T(8,128)S(1)}, f32[384,256]{0,1:T(8,128)S(1)}, u32[]{:S(2)}, u32[]{:S(2)}) collective-permute-start(f32[384,256]{0,1:T(8,128)S(1)} %get-tuple-element.28), channel_id=1, source_target_pairs={{1,0},{2,1},{3,2},{4,3},{5,4},{6,5},{7,6},{8,7},{9,8},{10,9},{11,1... | collective-permute-start | bytes 1179656 | tf_op jit(solution)/shard_map/ppermute | solution.py:12
  562.3 9.2 collective-permute-start.24
  565.6 9.4 collective-permute-start.25
  567.6 10.9 %collective-permute-start.26 = (f32[384,256]{0,1:T(8,128)S(1)}, f32[384,256]{0,1:T(8,128)S(1)}, u32[]{:S(2)}, u32[]{:S(2)}) collective-permute-start(f32[384,256]{0,1:T(8,128)S(1)} %get-tuple-element.25), channel_id=1, source_target_pairs={{0,1},{1,2},{2,3},{3,4},{4,5},{5,6},{6,7},{7,8},{8,9},{9,10},{10,1... | collective-permute-start | bytes 1179656 | tf_op jit(solution)/shard_map/ppermute | solution.py:12
  570.2 12.4 %collective-permute-start.27 = (f32[384,256]{0,1:T(8,128)S(1)}, f32[384,256]{0,1:T(8,128)S(1)}, u32[]{:S(2)}, u32[]{:S(2)}) collective-permute-start(f32[384,256]{0,1:T(8,128)S(1)} %get-tuple-element.24), channel_id=1, source_target_pairs={{1,0},{2,1},{3,2},{4,3},{5,4},{6,5},{7,6},{8,7},{9,8},{10,9},{11,1... | collective-permute-start | bytes 1179656 | tf_op jit(solution)/shard_map/ppermute | solution.py:12
  680.6 8.8 collective-permute-start.28
  684.6 9.4 collective-permute-start.29
  686.5 9.2 collective-permute-start.30
  687.8 12.0 %collective-permute-start.31 = (f32[384,256]{0,1:T(8,128)S(1)}, f32[384,256]{0,1:T(8,128)S(1)}, u32[]{:S(2)}, u32[]{:S(2)}) collective-permute-start(f32[384,256]{0,1:T(8,128)S(1)} %get-tuple-element.20), channel_id=1, source_target_pairs={{1,0},{2,1},{3,2},{4,3},{5,4},{6,5},{7,6},{8,7},{9,8},{10,9},{11,1... | collective-permute-start | bytes 1179656 | tf_op jit(solution)/shard_map/ppermute | solution.py:12
  878.0 20.3 %all-to-all-start.1 = ((f32[128,4,256]{2,1,0:T(4,128)}), f32[128,4,256]{2,1,0:T(4,128)}, u32[]{:S(2)}, u32[]{:S(2)}) async-start(f32[128,4,256]{2,1,0:T(4,128)} %stack.135), calls=%async_computation.1 | async-start | bytes 1048576 | tf_op jit(solution)/shard_map/all_to_all | solution.py:33
  897.5 6.4 copy-start.15
  906.5 9.6 collective-permute-start.32
  909.9 9.4 collective-permute-start.33
  911.8 10.4 %collective-permute-start.34 = (f32[384,256]{0,1:T(8,128)S(1)}, f32[384,256]{0,1:T(8,128)S(1)}, u32[]{:S(2)}, u32[]{:S(2)}) collective-permute-start(f32[384,256]{0,1:T(8,128)S(1)} %get-tuple-element.17), channel_id=1, source_target_pairs={{0,1},{1,2},{2,3},{3,4},{4,5},{5,6},{6,7},{7,8},{8,9},{9,10},{10,1... | collective-permute-start | bytes 1179656 | tf_op jit(solution)/shard_map/ppermute | solution.py:12
  914.5 11.9 %collective-permute-start.35 = (f32[384,256]{0,1:T(8,128)S(1)}, f32[384,256]{0,1:T(8,128)S(1)}, u32[]{:S(2)}, u32[]{:S(2)}) collective-permute-start(f32[384,256]{0,1:T(8,128)S(1)} %get-tuple-element.16), channel_id=1, source_target_pairs={{1,0},{2,1},{3,2},{4,3},{5,4},{6,5},{7,6},{8,7},{9,8},{10,9},{11,1... | collective-permute-start | bytes 1179656 | tf_op jit(solution)/shard_map/ppermute | solution.py:12
  (13 other events, 27.8 us)
Sparse Core Ops, SparseCore 0:
  203.9 150.5 all-reduce.5
  728.2 147.5 all-reduce.7
